TPU v7x, 128 devices: a whole 4x4x4 slice. The times are simulated.
128 devices in a mesh: section: 2 (over z_lo), dp: 16 (over y, x), tensor: 4 (over z_hi, core).
Axes of the slice: x: 4, y: 4, z: 4 (z_hi: 2, z_lo: 2; z = z_hi * 2 + z_lo), core: 2. Of those that a mesh axis runs over, the one named last changes fastest.
Arguments:
- images: bfloat16 [48, 577, 768], P('dp', None, 'tensor'), may hold values from -6 to 6
- slot_table: int32 [32], P('dp'), may hold values from 0 to 3, as said below
- ln1_gain: float32 [2, 768], P('section'), may hold values from 0.5 to 1.5
- ln1_bias: float32 [2, 768], P('section'), may hold values from -1.5 to 1.5
- qkv_weight: bfloat16 [2, 768, 3, 768], P('section', None, None, 'tensor'), may hold values from -0.21875 to 0.21875
- qv_bias: float32 [2, 2, 768], P('section', None, 'tensor'), may hold values from -1.5 to 1.5
- out_weight: bfloat16 [2, 768, 768], P('section', 'tensor'), may hold values from -0.875 to 0.875
- out_bias: float32 [2, 768], P('section'), may hold values from -1.5 to 1.5
- ln2_gain: float32 [2, 768], P('section'), may hold values from 0.5 to 1.5
- ln2_bias: float32 [2, 768], P('section'), may hold values from -1.5 to 1.5
- fc1_weight: bfloat16 [2, 768, 3072], P('section', None, 'tensor'), may hold values from -0.21875 to 0.21875
- fc1_bias: float32 [2, 3072], P('section', 'tensor'), may hold values from -1.5 to 1.5
- fc2_weight: bfloat16 [2, 3072, 768], P('section', 'tensor'), may hold values from -0.109375 to 0.109375
- fc2_bias: float32 [2, 768], P('section'), may hold values from -1.5 to 1.5
- cotangent: bfloat16 [48, 577, 768], P('dp', None, 'tensor'), may hold values from -6 to 6
Outputs:
- activations: bfloat16 [2, 48, 577, 768], P('section', 'dp', None, 'tensor')
- input_grads: float32 [2, 48, 577, 768], P('section', 'dp', None, 'tensor')
- ln1_gain_grad: float32 [2, 768], P('section', 'tensor')
- ln1_bias_grad: float32 [2, 768], P('section', 'tensor')
- qkv_weight_grad: float32 [2, 768, 3, 768], P('section', None, None, 'tensor')
- qv_bias_grad: float32 [2, 2, 768], P('section', None, 'tensor')
- out_weight_grad: float32 [2, 768, 768], P('section', 'tensor')
- out_bias_grad: float32 [2, 768], P('section', 'tensor')
- ln2_gain_grad: float32 [2, 768], P('section', 'tensor')
- ln2_bias_grad: float32 [2, 768], P('section', 'tensor')
- fc1_weight_grad: float32 [2, 768, 3072], P('section', None, 'tensor')
- fc1_bias_grad: float32 [2, 3072], P('section', 'tensor')
- fc2_weight_grad: float32 [2, 3072, 768], P('section', 'tensor')
- fc2_bias_grad: float32 [2, 768], P('section', 'tensor')
Inputs may be any that keep to these rules, and one draw needn't show every extreme that they name: `slot_table`: within one data member's 2 entries, values below 3 are distinct; the value 3 means that the micro-batch has no image there.
All inputs are finite; a program needn't handle non-finite values.
Results may differ from a plain program's by a relative error of at most 0.0095.
Values may be sent and summed in bfloat16 or wider, within the bound.
No kernel may reach another device: no remote copies, remote signals or barrier semaphores. Data moves between devices by JAX's collectives and lax.ppermute only.
A program may use at most 192 MiB of HBM per device.

v0:
```python
from functools import partial
import jax
import jax.numpy as jnp
from jax import lax
from jax.sharding import PartitionSpec as P

HD = 64
epsilon = 1e-06


def shifted(block, axis, distance):
    devices = range(lax.axis_size(axis))
    route = [(i - distance, i) for i in devices if i - distance in devices]
    return lax.ppermute(block, axis, route)


def standardize_rows(values):
    row_means = jnp.mean(values, axis=1, keepdims=True)
    center = values - row_means
    inverse = lax.rsqrt(jnp.mean(center * center, axis=1, keepdims=True) + epsilon)
    return (center * inverse, row_means, inverse)


def contract_rows(left_side, right_side):
    return lax.dot_general(
        left_side, right_side, (((0,), (0,)), ((), ())), preferred_element_type=jnp.float32
    )


def contract_cols(left_side, right_side):
    return lax.dot_general(
        left_side, right_side, (((1,), (1,)), ((), ())), preferred_element_type=jnp.float32
    )


def member_sum(gradients):
    return lax.psum(gradients, "dp")


def layer_forward(partial_residual, params, column):
    (
        first_norm_gain,
        first_norm_bias,
        qkv_mat,
        qv_add,
        out_mat,
        out_add,
        second_norm_gain,
        second_norm_bias,
        up_mat,
        up_add,
        down_mat,
        down_add,
    ) = params
    rows_count = partial_residual.shape[0]
    part_width = partial_residual.shape[1]
    hidden_width = first_norm_gain.shape[0]
    head_count = part_width // HD

    def local_part(vector):
        return lax.dynamic_slice_in_dim(vector, column, part_width, 0)

    complete_residual = lax.all_gather(partial_residual, "tensor", axis=1, tiled=True)
    first_centered_unit, first_row_averages, first_inverse_deviation = standardize_rows(
        complete_residual.astype(jnp.float32)
    )
    first_normalized = (first_centered_unit * first_norm_gain + first_norm_bias).astype(
        jnp.bfloat16
    )
    projected = jnp.dot(
        first_normalized,
        qkv_mat.reshape(hidden_width, 3 * part_width),
        preferred_element_type=jnp.float32,
    ).reshape(rows_count, 3, part_width)
    queries = (projected[:, 0] + qv_add[0]).astype(jnp.bfloat16).reshape(rows_count, head_count, HD)
    keys_part = projected[:, 1].astype(jnp.bfloat16).reshape(rows_count, head_count, HD)
    values_part = (
        (projected[:, 2] + qv_add[1]).astype(jnp.bfloat16).reshape(rows_count, head_count, HD)
    )
    scores = jnp.einsum(
        "qhd,khd->hqk", queries, keys_part, preferred_element_type=jnp.float32
    ) * HD ** (-0.5)
    totals = jax.nn.logsumexp(scores, axis=2, keepdims=True)
    probabilities = jnp.exp(scores - totals)
    attended = (
        jnp.einsum(
            "hqk,khd->qhd",
            probabilities.astype(jnp.bfloat16),
            values_part,
            preferred_element_type=jnp.float32,
        )
        .reshape(rows_count, part_width)
        .astype(jnp.bfloat16)
    )
    branch = lax.psum_scatter(
        jnp.dot(attended, out_mat, preferred_element_type=jnp.float32),
        "tensor",
        scatter_dimension=1,
        tiled=True,
    )
    middle = partial_residual.astype(jnp.float32) + branch + local_part(out_add)
    complete_middle_state = lax.all_gather(
        middle.astype(jnp.bfloat16), "tensor", axis=1, tiled=True
    )
    second_centered_unit, second_row_averages, second_inverse_deviation = standardize_rows(
        complete_middle_state.astype(jnp.float32)
    )
    second_normalized = (second_centered_unit * second_norm_gain + second_norm_bias).astype(
        jnp.bfloat16
    )
    hidden_pre = jnp.dot(second_normalized, up_mat, preferred_element_type=jnp.float32) + up_add
    hidden = jax.nn.gelu(hidden_pre, approximate=False).astype(jnp.bfloat16)
    feed_out = lax.psum_scatter(
        jnp.dot(hidden, down_mat, preferred_element_type=jnp.float32),
        "tensor",
        scatter_dimension=1,
        tiled=True,
    )
    result = middle + feed_out + local_part(down_add)
    saved_state = (
        partial_residual,
        first_row_averages,
        first_inverse_deviation,
        first_normalized,
        queries,
        keys_part,
        values_part,
        totals,
        attended,
        complete_middle_state,
        second_row_averages,
        second_inverse_deviation,
        second_normalized,
        hidden_pre,
        hidden,
    )
    return (result.astype(jnp.bfloat16), saved_state)


def layer_backward(grad_part, saved_state, params, column, grad_sums):
    (
        first_norm_gain,
        first_norm_bias,
        qkv_mat,
        qv_add,
        out_mat,
        out_add,
        second_norm_gain,
        second_norm_bias,
        up_mat,
        up_add,
        down_mat,
        down_add,
    ) = params
    (
        partial_residual,
        first_row_averages,
        first_inverse_deviation,
        first_normalized,
        queries,
        keys_part,
        values_part,
        totals,
        attended,
        complete_middle_state,
        second_row_averages,
        second_inverse_deviation,
        second_normalized,
        hidden_pre,
        hidden,
    ) = saved_state
    rows_count = grad_part.shape[0]
    part_width = grad_part.shape[1]
    hidden_width = first_norm_gain.shape[0]
    head_count = part_width // HD

    def local_part(vector):
        return lax.dynamic_slice_in_dim(vector, column, part_width, 0)

    grad_full = lax.all_gather(grad_part.astype(jnp.bfloat16), "tensor", axis=1, tiled=True)
    down_grad = contract_rows(hidden, grad_full)
    down_add_grad = jnp.sum(grad_part, axis=0)
    hidden_grad = contract_cols(grad_full, down_mat)
    unused_value, gelu_back = jax.vjp(partial(jax.nn.gelu, approximate=False), hidden_pre)
    pre_grad = gelu_back(hidden_grad)[0].astype(jnp.bfloat16)
    up_grad = contract_rows(second_normalized, pre_grad)
    up_add_grad = jnp.sum(pre_grad.astype(jnp.float32), axis=0)
    normalized_gradient = lax.psum_scatter(
        contract_cols(pre_grad, up_mat), "tensor", scatter_dimension=1, tiled=True
    )
    local_middle_state = lax.dynamic_slice_in_dim(
        complete_middle_state, column, part_width, 1
    ).astype(jnp.float32)
    second_centered_unit = (local_middle_state - second_row_averages) * second_inverse_deviation
    second_gain_gradient = jnp.sum(normalized_gradient * second_centered_unit, axis=0)
    bias_two_grad = jnp.sum(normalized_gradient, axis=0)
    second_rescaled = normalized_gradient * local_part(second_norm_gain)
    first_running_total, second_running_total = lax.psum(
        (
            jnp.sum(second_rescaled, axis=1, keepdims=True),
            jnp.sum(second_rescaled * second_centered_unit, axis=1, keepdims=True),
        ),
        "tensor",
    )
    middle_grad = grad_part + second_inverse_deviation * (
        second_rescaled
        - first_running_total / hidden_width
        - second_centered_unit * second_running_total / hidden_width
    )
    feed_grads = (
        second_gain_gradient,
        bias_two_grad,
        up_grad,
        up_add_grad,
        down_grad,
        down_add_grad,
    )
    feed_grads = tuple((older + newer for older, newer in zip(grad_sums[6:], feed_grads)))
    branch_grad = lax.all_gather(middle_grad.astype(jnp.bfloat16), "tensor", axis=1, tiled=True)
    out_grad = contract_rows(attended, branch_grad)
    out_add_grad = jnp.sum(middle_grad, axis=0)
    attended_grad = (
        contract_cols(branch_grad, out_mat).astype(jnp.bfloat16).reshape(rows_count, head_count, HD)
    )
    scale_factor = HD ** (-0.5)
    scores = (
        jnp.einsum("qhd,khd->hqk", queries, keys_part, preferred_element_type=jnp.float32)
        * scale_factor
    )
    probabilities = jnp.exp(scores - totals)
    values_grad = jnp.einsum(
        "hqk,qhd->khd",
        probabilities.astype(jnp.bfloat16),
        attended_grad,
        preferred_element_type=jnp.float32,
    )
    weight_grad = jnp.einsum(
        "qhd,khd->hqk", attended_grad, values_part, preferred_element_type=jnp.float32
    )
    rowdot = jnp.sum(probabilities * weight_grad, axis=2, keepdims=True)
    score_grad = (probabilities * (weight_grad - rowdot)).astype(jnp.bfloat16)
    query_grad = (
        jnp.einsum("hqk,khd->qhd", score_grad, keys_part, preferred_element_type=jnp.float32)
        * scale_factor
    )
    key_grad = (
        jnp.einsum("hqk,qhd->khd", score_grad, queries, preferred_element_type=jnp.float32)
        * scale_factor
    )
    projected_grad = jnp.stack(
        [
            query_grad.reshape(rows_count, part_width),
            key_grad.reshape(rows_count, part_width),
            values_grad.reshape(rows_count, part_width),
        ],
        axis=1,
    ).astype(jnp.bfloat16)
    flat_grad = projected_grad.reshape(rows_count, 3 * part_width)
    qkv_grad = contract_rows(first_normalized, flat_grad).reshape(hidden_width, 3, part_width)
    qv_add_grad = jnp.stack(
        [
            jnp.sum(projected_grad[:, 0].astype(jnp.float32), axis=0),
            jnp.sum(projected_grad[:, 2].astype(jnp.float32), axis=0),
        ]
    )
    first_normalized_gradient = lax.psum_scatter(
        contract_cols(flat_grad, qkv_mat.reshape(hidden_width, 3 * part_width)),
        "tensor",
        scatter_dimension=1,
        tiled=True,
    )
    first_centered_unit = (
        partial_residual.astype(jnp.float32) - first_row_averages
    ) * first_inverse_deviation
    first_gain_gradient = jnp.sum(first_normalized_gradient * first_centered_unit, axis=0)
    bias_one_grad = jnp.sum(first_normalized_gradient, axis=0)
    first_rescaled = first_normalized_gradient * local_part(first_norm_gain)
    third_running_total, fourth_running_total = lax.psum(
        (
            jnp.sum(first_rescaled, axis=1, keepdims=True),
            jnp.sum(first_rescaled * first_centered_unit, axis=1, keepdims=True),
        ),
        "tensor",
    )
    stream_grad = middle_grad + first_inverse_deviation * (
        first_rescaled
        - third_running_total / hidden_width
        - first_centered_unit * fourth_running_total / hidden_width
    )
    attention_grads = (
        first_gain_gradient,
        bias_one_grad,
        qkv_grad,
        qv_add_grad,
        out_grad,
        out_add_grad,
    )
    attention_grads = tuple((older + newer for older, newer in zip(grad_sums[:6], attention_grads)))
    return (stream_grad, attention_grads + feed_grads)


def shards(
    images,
    slot_table,
    ln1_gain,
    ln1_bias,
    qkv_weight,
    qv_bias,
    out_weight,
    out_bias,
    ln2_gain,
    ln2_bias,
    fc1_weight,
    fc1_bias,
    fc2_weight,
    fc2_bias,
    cotangent,
):
    params = tuple(
        (
            weight_arg[0]
            for weight_arg in (
                ln1_gain,
                ln1_bias,
                qkv_weight,
                qv_bias,
                out_weight,
                out_bias,
                ln2_gain,
                ln2_bias,
                fc1_weight,
                fc1_bias,
                fc2_weight,
                fc2_bias,
            )
        )
    )
    section_index = lax.axis_index("section")
    part_width = images.shape[2]
    column = lax.axis_index("tensor") * part_width
    slot_count = images.shape[0]
    micro_count = slot_table.shape[0]
    slot_ids = jnp.arange(slot_count, dtype=jnp.int32)

    def locate(batch_index):
        clipped = jnp.clip(batch_index, 0, micro_count - 1)
        chosen = lax.dynamic_index_in_dim(slot_table, clipped, 0, keepdims=False)
        active = (batch_index >= 0) & (batch_index < micro_count) & (chosen < slot_count)
        return (jnp.minimum(chosen, slot_count - 1), active, (slot_ids == chosen) & active)

    received = jnp.zeros(images.shape[1:], jnp.bfloat16)
    layer_outputs = jnp.zeros(images.shape, jnp.bfloat16)
    saved_states = []
    for step_index in range(micro_count + 1):
        where_from, active, placed = locate(step_index - section_index)
        own_image = lax.dynamic_index_in_dim(images, where_from, 0, keepdims=False)
        entering = jnp.where(section_index == 0, own_image, received)
        leaving, layer_state = layer_forward(entering, params, column)
        saved_states.append(layer_state)
        layer_outputs = layer_outputs + placed[:, None, None].astype(jnp.bfloat16) * leaving[None]
        if step_index < micro_count:
            received = shifted(leaving, "section", 1)

    def zeros_of(extent):
        return jnp.zeros(extent, jnp.float32)

    grad_sums = (
        zeros_of((part_width,)),
        zeros_of((part_width,)),
        zeros_of(params[2].shape),
        zeros_of(params[3].shape),
        zeros_of(params[4].shape),
        zeros_of((part_width,)),
        zeros_of((part_width,)),
        zeros_of((part_width,)),
        zeros_of(params[8].shape),
        zeros_of(params[9].shape),
        zeros_of(params[10].shape),
        zeros_of((part_width,)),
    )
    coming_back = jnp.zeros(images.shape[1:], jnp.bfloat16)
    grads_in = jnp.zeros(images.shape, jnp.float32)
    for step_index in range(micro_count + 1):
        where_from, active, placed = locate(micro_count - step_index - section_index)
        own_grad = lax.dynamic_index_in_dim(cotangent, where_from, 0, keepdims=False)
        entering = jnp.where(section_index == 1, own_grad, coming_back).astype(
            jnp.float32
        ) * active.astype(jnp.float32)
        stream_grad, grad_sums = layer_backward(
            entering, saved_states[micro_count - step_index], params, column, grad_sums
        )
        grads_in = grads_in + placed[:, None, None].astype(jnp.float32) * stream_grad[None]
        if step_index < micro_count:
            coming_back = shifted(stream_grad.astype(jnp.bfloat16), "section", -1)
    grad_sums = member_sum(grad_sums)
    return (layer_outputs[None], grads_in[None]) + tuple((gradient[None] for gradient in grad_sums))


def solution(mesh):
    in_specs = (
        P("dp", None, "tensor"),
        P("dp"),
        P("section", None),
        P("section", None),
        P("section", None, None, "tensor"),
        P("section", None, "tensor"),
        P("section", "tensor", None),
        P("section", None),
        P("section", None),
        P("section", None),
        P("section", None, "tensor"),
        P("section", "tensor"),
        P("section", "tensor", None),
        P("section", None),
        P("dp", None, "tensor"),
    )
    out_specs = (
        P("section", "dp", None, "tensor"),
        P("section", "dp", None, "tensor"),
        P("section", "tensor"),
        P("section", "tensor"),
        P("section", None, None, "tensor"),
        P("section", None, "tensor"),
        P("section", "tensor", None),
        P("section", "tensor"),
        P("section", "tensor"),
        P("section", "tensor"),
        P("section", None, "tensor"),
        P("section", "tensor"),
        P("section", "tensor", None),
        P("section", "tensor"),
    )
    return jax.shard_map(shards, mesh=mesh, in_specs=in_specs, out_specs=out_specs, check_vma=False)
```

profile of v0, /device:TPU:1, one launch (start us, length us, event | category | flops | bytes accessed | tf_op | source)
XLA Modules:
  0.0 948.7 jit_solution(2319730954363733079)
XLA Ops:
  10.3 13.4 %all-gather = bf16[1,577,768]{1,2,0:T(8,128)(2,1)S(1)} all-gather(bf16[1,577,192]{1,2,0:T(8,128)(2,1)S(1)} %dynamic-slice_select_fusion.1), channel_id=2, replica_groups=mesh['section'=2,'dp'=16,'tensor'=4] {'tensor'}, dimensions={2}, use_global_device_ids=true | all-gather | bytes 1107840 | tf_op jit(solution)/shard_map/all_gather | solution.py:63
  30.3 3.3 convolution_convert_fusion.5
  36.4 37.5 %reduce-scatter.13.cloned.1.call-done = f32[577,192]{0,1:T(8,128)} async-done(((f32[577,768]{0,1:T(8,128)}), f32[577,192]{0,1:T(8,128)}) %reduce-scatter.13.cloned.1.call-update) | async-done | bytes 443152 | tf_op jit(solution)/shard_map/reduce_scatter | solution.py:95
  75.1 11.5 %all_gather.37 = bf16[577,768]{0,1:T(8,128)(2,1)S(1)} all-gather(bf16[577,192]{0,1:T(8,128)(2,1)S(1)} %fusion.150), channel_id=1, replica_groups=mesh['section'=2,'dp'=16,'tensor'=4] {'tensor'}, dimensions={1}, use_global_device_ids=true | all-gather | bytes 1107840 | tf_op jit(solution)/shard_map/all_gather | solution.py:102
  87.1 6.5 multiply_convert_fusion.5
  97.9 35.8 %reduce-scatter.15.cloned.1.call-done = f32[577,192]{0,1:T(8,128)} async-done(((f32[577,768]{0,1:T(8,128)}), f32[577,192]{0,1:T(8,128)}) %reduce-scatter.15.cloned.1.call-update) | async-done | bytes 443152 | tf_op jit(solution)/shard_map/reduce_scatter | solution.py:113
  135.0 3.0 collective-permute-start
  138.6 3.3 collective-permute-done
  141.9 11.8 %all_gather.38 = bf16[577,768]{0,1:T(8,128)(2,1)S(1)} all-gather(bf16[577,192]{0,1:T(8,128)(2,1)S(1)} %bitcast_select_fusion.3), channel_id=1, replica_groups=mesh['section'=2,'dp'=16,'tensor'=4] {'tensor'}, dimensions={1}, use_global_device_ids=true | all-gather | bytes 1107840 | tf_op jit(solution)/shard_map/all_gather | solution.py:63
  161.4 39.7 %reduce-scatter.17.cloned.1.call-done = f32[577,192]{0,1:T(8,128)} async-done(((f32[577,768]{0,1:T(8,128)}), f32[577,192]{0,1:T(8,128)}) %reduce-scatter.17.cloned.1.call-update) | async-done | bytes 443152 | tf_op jit(solution)/shard_map/reduce_scatter | solution.py:95
  202.3 11.3 %all_gather.39 = bf16[577,768]{0,1:T(8,128)(2,1)S(1)} all-gather(bf16[577,192]{0,1:T(8,128)(2,1)S(1)} %fusion.152), channel_id=1, replica_groups=mesh['section'=2,'dp'=16,'tensor'=4] {'tensor'}, dimensions={1}, use_global_device_ids=true | all-gather | bytes 1107840 | tf_op jit(solution)/shard_map/all_gather | solution.py:102
  214.1 6.5 multiply_convert_fusion.4
  224.6 36.0 %reduce-scatter.19.cloned.1.call-done = f32[577,192]{0,1:T(8,128)} async-done(((f32[577,768]{0,1:T(8,128)}), f32[577,192]{0,1:T(8,128)}) %reduce-scatter.19.cloned.1.call-update) | async-done | bytes 443152 | tf_op jit(solution)/shard_map/reduce_scatter | solution.py:113
  266.4 3.6 collective-permute-done.1
  271.6 11.5 %all_gather.40 = bf16[577,768]{0,1:T(8,128)(2,1)S(1)} all-gather(bf16[577,192]{0,1:T(8,128)(2,1)S(1)} %bitcast_select_fusion.2), channel_id=1, replica_groups=mesh['section'=2,'dp'=16,'tensor'=4] {'tensor'}, dimensions={1}, use_global_device_ids=true | all-gather | bytes 1107840 | tf_op jit(solution)/shard_map/all_gather | solution.py:63
  293.9 11.7 %all_gather.42 = bf16[577,768]{0,1:T(8,128)(2,1)} all-gather(bf16[577,192]{0,1:T(8,128)(2,1)S(1)} %get-tuple-element.97), channel_id=1, replica_groups=mesh['section'=2,'dp'=16,'tensor'=4] {'tensor'}, dimensions={1}, use_global_device_ids=true | all-gather | bytes 1107840 | tf_op jit(solution)/shard_map/all_gather | solution.py:180
  305.6 24.8 %reduce-scatter.21.cloned.1.call-done = f32[577,192]{0,1:T(8,128)} async-done(((f32[577,768]{0,1:T(8,128)}), f32[577,192]{0,1:T(8,128)}) %reduce-scatter.21.cloned.1.call-update) | async-done | bytes 443152 | tf_op jit(solution)/shard_map/reduce_scatter | solution.py:95
  331.6 11.3 %all_gather.41 = bf16[577,768]{0,1:T(8,128)(2,1)S(1)} all-gather(bf16[577,192]{0,1:T(8,128)(2,1)S(1)} %fusion.151), channel_id=1, replica_groups=mesh['section'=2,'dp'=16,'tensor'=4] {'tensor'}, dimensions={1}, use_global_device_ids=true | all-gather | bytes 1107840 | tf_op jit(solution)/shard_map/all_gather | solution.py:102
  343.5 5.7 multiply_convert_fusion.3
  355.4 35.7 %reduce-scatter.25.cloned.1.call-done = f32[577,192]{0,1:T(8,128)} async-done(((f32[577,768]{0,1:T(8,128)}), f32[577,192]{0,1:T(8,128)}) %reduce-scatter.25.cloned.1.call-update) | async-done | bytes 443152 | tf_op jit(solution)/shard_map/reduce_scatter | solution.py:188
  393.7 8.0 all-reduce.7
  404.6 12.2 %all_gather.43 = bf16[577,768]{0,1:T(8,128)(2,1)S(1)} all-gather(bf16[577,192]{0,1:T(8,128)(2,1)S(1)} %convert_element_type.415), channel_id=1, replica_groups=mesh['section'=2,'dp'=16,'tensor'=4] {'tensor'}, dimensions={1}, use_global_device_ids=true | all-gather | bytes 1107840 | tf_op jit(solution)/shard_map/all_gather | solution.py:219
  417.8 3.6 multiply_reduce_fusion.2
  429.3 4.0 fusion.65
  434.1 31.7 %reduce-scatter.27.cloned.1.call-done = f32[577,192]{0,1:T(8,128)} async-done(((f32[577,768]{0,1:T(8,128)}), f32[577,192]{0,1:T(8,128)}) %reduce-scatter.27.cloned.1.call-update) | async-done | bytes 443152 | tf_op jit(solution)/shard_map/reduce_scatter | solution.py:266
  468.3 7.9 all-reduce.6
  476.9 29.2 %reduce-scatter.23.cloned.1.call-done = f32[577,192]{0,1:T(8,128)} async-done(((f32[577,768]{0,1:T(8,128)}), f32[577,192]{0,1:T(8,128)}) %reduce-scatter.23.cloned.1.call-update) | async-done | bytes 443152 | tf_op jit(solution)/shard_map/reduce_scatter | solution.py:113
  511.0 7.1 collective-permute-done.2
  520.7 11.3 %all_gather.44 = bf16[577,768]{0,1:T(8,128)(2,1)S(1)} all-gather(bf16[577,192]{0,1:T(8,128)(2,1)S(1)} %fusion.139), channel_id=1, replica_groups=mesh['section'=2,'dp'=16,'tensor'=4] {'tensor'}, dimensions={1}, use_global_device_ids=true | all-gather | bytes 1107840 | tf_op jit(solution)/shard_map/all_gather | solution.py:180
  532.0 4.5 convert_reduce_fusion.7
  539.8 37.2 %reduce-scatter.29.cloned.1.call-done = f32[577,192]{0,1:T(8,128)} async-done(((f32[577,768]{0,1:T(8,128)}), f32[577,192]{0,1:T(8,128)}) %reduce-scatter.29.cloned.1.call-update) | async-done | bytes 443152 | tf_op jit(solution)/shard_map/reduce_scatter | solution.py:188
  578.9 7.3 all-reduce.5
  588.3 12.5 %all_gather.45 = bf16[577,768]{0,1:T(8,128)(2,1)S(1)} all-gather(bf16[577,192]{0,1:T(8,128)(2,1)S(1)} %convert_element_type.427), channel_id=1, replica_groups=mesh['section'=2,'dp'=16,'tensor'=4] {'tensor'}, dimensions={1}, use_global_device_ids=true | all-gather | bytes 1107840 | tf_op jit(solution)/shard_map/all_gather | solution.py:219
  601.7 3.6 multiply_reduce_fusion.1
  613.3 36.5 %reduce-scatter.31.cloned.1.call-done = f32[577,192]{0,1:T(8,128)} async-done(((f32[577,768]{0,1:T(8,128)}), f32[577,192]{0,1:T(8,128)}) %reduce-scatter.31.cloned.1.call-update) | async-done | bytes 443152 | tf_op jit(solution)/shard_map/reduce_scatter | solution.py:266
  651.7 7.3 all-reduce.4
  663.3 7.1 collective-permute-done.3
  672.4 11.4 %all_gather.46 = bf16[577,768]{0,1:T(8,128)(2,1)S(1)} all-gather(bf16[577,192]{0,1:T(8,128)(2,1)S(1)} %fusion.137), channel_id=1, replica_groups=mesh['section'=2,'dp'=16,'tensor'=4] {'tensor'}, dimensions={1}, use_global_device_ids=true | all-gather | bytes 1107840 | tf_op jit(solution)/shard_map/all_gather | solution.py:180
  683.7 3.9 convert_reduce_fusion.6
  691.1 4.1 fusion.191
  695.1 33.1 %reduce-scatter.33.cloned.1.call-done = f32[577,192]{0,1:T(8,128)} async-done(((f32[577,768]{0,1:T(8,128)}), f32[577,192]{0,1:T(8,128)}) %reduce-scatter.33.cloned.1.call-update) | async-done | bytes 443152 | tf_op jit(solution)/shard_map/reduce_scatter | solution.py:188
  730.2 7.2 all-reduce.3
  738.9 12.1 %all_gather.47 = bf16[577,768]{0,1:T(8,128)(2,1)S(1)} all-gather(bf16[577,192]{0,1:T(8,128)(2,1)S(1)} %convert_element_type.439), channel_id=1, replica_groups=mesh['section'=2,'dp'=16,'tensor'=4] {'tensor'}, dimensions={1}, use_global_device_ids=true | all-gather | bytes 1107840 | tf_op jit(solution)/shard_map/all_gather | solution.py:219
  751.9 3.6 multiply_reduce_fusion
  789.0 11.0 %reduce-scatter.35.cloned.1.call-done = f32[577,192]{0,1:T(8,128)} async-done(((f32[577,768]{0,1:T(8,128)}), f32[577,192]{0,1:T(8,128)}) %reduce-scatter.35.cloned.1.call-update) | async-done | bytes 443152 | tf_op jit(solution)/shard_map/reduce_scatter | solution.py:266
  801.4 62.2 %all-reduce = (f32[1,192]{1,0:T(1,128)}, f32[1,192]{1,0:T(1,128)}, f32[1,2,192]{2,1,0:T(2,128)}, f32[1,192]{1,0:T(1,128)}, f32[1,192]{1,0:T(1,128)}, /*index=5*/...) all-reduce(f32[1,192]{1,0:T(1,128)S(1)} %bitcast.365, ...), channel_id=1, replica_groups=mesh['section'=2,'dp'=16,'tensor'=4] {'dp'}, use_global_device_ids=true, to_apply=%region_60.61 | all-reduce | flops 2304 | bytes 18432 | tf_op jit(solution)/shard_map/psum | solution.py:37
  863.6 20.7 %all-reduce.2 = (f32[577]{0:T(1024)S(1)}, f32[577,1]{0,1:T(1,128)S(1)}) all-reduce(f32[577]{0:T(1024)S(1)} %get-tuple-element.25, f32[577,1]{0,1:T(1,128)S(1)} %broadcast_in_dim.58), channel_id=1, replica_groups=mesh['section'=2,'dp'=16,'tensor'=4] {'tensor'}, use_global_device_ids=true, to_apply=%region_56.57 | all-reduce | flops 1154 | bytes 9232 | tf_op jit(solution)/shard_map/psum | solution.py:278
  888.1 46.2 %all-reduce.10.cloned.1.call-done = (f32[1,768,3,192]{1,3,2,0:T(8,128)}, f32[1,192,768]{2,1,0:T(8,128)}, f32[1,768,768]{2,1,0:T(8,128)}, f32[1,768,768]{2,1,0:T(8,128)}) async-done(((f32[1,768,3,192]{1,3,2,0:T(8,128)}, f32[1,192,768]{2,1,0:T(8,128)}, f32[1,768,768]{2,1,0:T(8,128)}, f32[1,768,768]{2,1,0:T(8,128)}), (f32[1,768,3,192]{1,3,2,0:T(8,128)}, f32[1,192,768]{2,1,0:T(8,128)}, ...) | async-done | bytes 7077904 | tf_op jit(solution)/shard_map/psum | solution.py:37
  (480 shorter events, 158.5 us)
Async XLA Ops:
  7.2 79.9 %copy-start = (bf16[1,768,768]{2,1,0:T(8,128)(2,1)S(1)}, bf16[1,768,768]{2,1,0:T(8,128)(2,1)}, u32[]{:S(2)}) copy-start(bf16[1,768,768]{2,1,0:T(8,128)(2,1)} %param.25) | copy-start | bytes 3538948
  7.2 66.7 %reduce-scatter.13.cloned.1.call-start = ((), (), s32[]{:S(2)}) async-start(), calls=%async_computation.12 | async-start | bytes 2457600 | tf_op jit(solution)/shard_map/reduce_scatter | solution.py:95
  9.3 14.9 %copy-start.93 = (f32[1,768]{1,0:T(1,128)S(1)}, f32[1,768]{1,0:T(1,128)}, u32[]{:S(2)}) copy-start(f32[1,768]{1,0:T(1,128)} %param.17) | copy-start | bytes 9220
  9.3 14.9 %copy-start.119 = (f32[1,768]{1,0:T(1,128)S(1)}, f32[1,768]{1,0:T(1,128)}, u32[]{:S(2)}) copy-start(f32[1,768]{1,0:T(1,128)} %param.18) | copy-start | bytes 9220
  24.2 259.5 %copy-start.101 = (f32[768]{0:T(1024)}, f32[768]{0:T(1024)S(1)}, u32[]{:S(2)}) copy-start(f32[768]{0:T(1024)S(1)} %reduce.8) | copy-start | bytes 9220
  24.3 130.0 %copy-start.103 = (f32[768]{0:T(1024)}, f32[768]{0:T(1024)S(1)}, u32[]{:S(2)}) copy-start(f32[768]{0:T(1024)S(1)} %reduce.9) | copy-start | bytes 9220
  33.7 40.3 %copy-start.36 = (bf16[3,577,192]{1,2,0:T(8,128)(2,1)S(1)}, bf16[3,577,192]{1,2,0:T(8,128)(2,1)}, u32[]{:S(2)}) copy-start(bf16[3,577,192]{1,2,0:T(8,128)(2,1)} %param.15) | copy-start | bytes 1994116
  35.5 98.2 %reduce-scatter.15.cloned.1.call-start = ((), (), s32[]{:S(2)}) async-start(), calls=%async_computation.13 | async-start | bytes 2457600 | tf_op jit(solution)/shard_map/reduce_scatter | solution.py:113
  35.6 178.5 %copy-start.106 = (f32[768]{0:T(1024)}, f32[768]{0:T(1024)S(1)}, u32[]{:S(2)}) copy-start(f32[768]{0:T(1024)S(1)} %reduce.14) | copy-start | bytes 9220
  87.1 7.5 copy-start.123
  97.1 104.1 %reduce-scatter.17.cloned.1.call-start = ((), (), s32[]{:S(2)}) async-start(), calls=%async_computation.14 | async-start | bytes 2457600 | tf_op jit(solution)/shard_map/reduce_scatter | solution.py:95
  135.0 6.9 collective-permute-start
  141.9 59.3 %copy-start.6 = (bf16[577,192]{0,1:T(8,128)(2,1)}, bf16[577,192]{0,1:T(8,128)(2,1)S(1)}, u32[]{:S(2)}) copy-start(bf16[577,192]{0,1:T(8,128)(2,1)S(1)} %bitcast_select_fusion.3) | copy-start | bytes 664708
  141.9 12.3 %copy-start.128 = (bf16[1,768,3,192]{1,3,2,0:T(8,128)(2,1)S(1)}, bf16[1,768,3,192]{1,3,2,0:T(8,128)(2,1)}, u32[]{:S(2)}) copy-start(bf16[1,768,3,192]{1,3,2,0:T(8,128)(2,1)} %param.19) | copy-start | bytes 2654212
  161.4 99.3 %reduce-scatter.19.cloned.1.call-start = ((), (), s32[]{:S(2)}) async-start(), calls=%async_computation.15 | async-start | bytes 2457600 | tf_op jit(solution)/shard_map/reduce_scatter | solution.py:113
  214.1 7.5 copy-start.124
  224.1 106.3 %reduce-scatter.21.cloned.1.call-start = ((), (), s32[]{:S(2)}) async-start(), calls=%async_computation.16 | async-start | bytes 2457600 | tf_op jit(solution)/shard_map/reduce_scatter | solution.py:95
  262.8 7.2 collective-permute-start.1
  271.6 12.1 %copy-start.104 = (f32[768]{0:T(1024)S(1)}, f32[768]{0:T(1024)}, u32[]{:S(2)}) copy-start(f32[768]{0:T(1024)} %copy-done.103) | copy-start | bytes 9220
  271.6 12.1 %copy-start.129 = (bf16[1,768,3,192]{1,3,2,0:T(8,128)(2,1)S(1)}, bf16[1,768,3,192]{1,3,2,0:T(8,128)(2,1)}, u32[]{:S(2)}) copy-start(bf16[1,768,3,192]{1,3,2,0:T(8,128)(2,1)} %param.19) | copy-start | bytes 2654212
  291.5 99.6 %reduce-scatter.25.cloned.1.call-start = ((), (), s32[]{:S(2)}) async-start(), calls=%async_computation.18 | async-start | bytes 2457600 | tf_op jit(solution)/shard_map/reduce_scatter | solution.py:188
  331.6 11.8 %copy-start.107 = (f32[768]{0:T(1024)S(1)}, f32[768]{0:T(1024)}, u32[]{:S(2)}) copy-start(f32[768]{0:T(1024)} %copy-done.106) | copy-start | bytes 9220
  354.6 111.2 %reduce-scatter.27.cloned.1.call-start = ((), (), s32[]{:S(2)}) async-start(), calls=%async_computation.19 | async-start | bytes 2457600 | tf_op jit(solution)/shard_map/reduce_scatter | solution.py:266
  404.6 12.7 %copy-start.20 = (f32[577,192]{0,1:T(8,128)}, f32[577,192]{0,1:T(8,128)S(1)}, u32[]{:S(2)}) copy-start(f32[577,192]{0,1:T(8,128)S(1)} %get-tuple-element.77) | copy-start | bytes 1329412
  404.6 13.2 %copy-start.35 = (f32[577,1,192]{0,2,1:T(8,128)S(1)}, f32[577,1,192]{0,2,1:T(8,128)}, u32[]{:S(2)}) copy-start(f32[577,1,192]{0,2,1:T(8,128)} %copy-done.34) | copy-start | bytes 1329412
  429.2 76.9 %reduce-scatter.23.cloned.1.call-start = ((), (), s32[]{:S(2)}) async-start(), calls=%async_computation.17 | async-start | bytes 2457600 | tf_op jit(solution)/shard_map/reduce_scatter | solution.py:113
  433.3 143.7 %reduce-scatter.29.cloned.1.call-start = ((), (), s32[]{:S(2)}) async-start(), calls=%async_computation.20 | async-start | bytes 2457600 | tf_op jit(solution)/shard_map/reduce_scatter | solution.py:188
  509.0 23.0 %copy-start.108 = (f32[768]{0:T(1024)S(1)}, f32[768]{0:T(1024)}, u32[]{:S(2)}) copy-start(f32[768]{0:T(1024)} %copy-done.106) | copy-start | bytes 9220
  509.0 9.2 collective-permute-start.2
  511.0 20.9 %copy-start.126 = (bf16[1,768,768]{2,1,0:T(8,128)(2,1)S(1)}, bf16[1,768,768]{2,1,0:T(8,128)(2,1)}, u32[]{:S(2)}) copy-start(bf16[1,768,768]{2,1,0:T(8,128)(2,1)} %param.27) | copy-start | bytes 3538948
  539.8 110.0 %reduce-scatter.31.cloned.1.call-start = ((), (), s32[]{:S(2)}) async-start(), calls=%async_computation.21 | async-start | bytes 2457600 | tf_op jit(solution)/shard_map/reduce_scatter | solution.py:266
  588.2 12.9 %copy-start.21 = (f32[577,192]{0,1:T(8,128)}, f32[577,192]{0,1:T(8,128)S(1)}, u32[]{:S(2)}) copy-start(f32[577,192]{0,1:T(8,128)S(1)} %get-tuple-element.75) | copy-start | bytes 1329412
  588.2 13.5 %copy-start.29 = (f32[577,1,192]{0,2,1:T(8,128)S(1)}, f32[577,1,192]{0,2,1:T(8,128)}, u32[]{:S(2)}) copy-start(f32[577,1,192]{0,2,1:T(8,128)} %copy-done.28) | copy-start | bytes 1329412
  613.2 115.1 %reduce-scatter.33.cloned.1.call-start = ((), (), s32[]{:S(2)}) async-start(), calls=%async_computation.22 | async-start | bytes 2457600 | tf_op jit(solution)/shard_map/reduce_scatter | solution.py:188
  659.1 24.7 %copy-start.109 = (f32[768]{0:T(1024)S(1)}, f32[768]{0:T(1024)}, u32[]{:S(2)}) copy-start(f32[768]{0:T(1024)} %copy-done.106) | copy-start | bytes 9220
  661.4 9.0 collective-permute-start.3
  663.3 20.5 %copy-start.127 = (bf16[1,768,768]{2,1,0:T(8,128)(2,1)S(1)}, bf16[1,768,768]{2,1,0:T(8,128)(2,1)}, u32[]{:S(2)}) copy-start(bf16[1,768,768]{2,1,0:T(8,128)(2,1)} %param.27) | copy-start | bytes 3538948
  691.0 109.0 %reduce-scatter.35.cloned.1.call-start = ((), (), s32[]{:S(2)}) async-start(), calls=%async_computation.23 | async-start | bytes 2457600 | tf_op jit(solution)/shard_map/reduce_scatter | solution.py:266
  738.9 12.5 %copy-start.30 = (f32[577,192]{0,1:T(8,128)}, f32[577,192]{0,1:T(8,128)S(1)}, u32[]{:S(2)}) copy-start(f32[577,192]{0,1:T(8,128)S(1)} %get-tuple-element.79) | copy-start | bytes 1329412
  738.9 13.1 %copy-start.25 = (f32[577,1,192]{0,2,1:T(8,128)S(1)}, f32[577,1,192]{0,2,1:T(8,128)}, u32[]{:S(2)}) copy-start(f32[577,1,192]{0,2,1:T(8,128)} %copy-done.24) | copy-start | bytes 1329412
  763.4 170.9 %all-reduce.10.cloned.1.call-start = ((), (), s32[]{:S(2)}) async-start(), calls=%async_computation.24 | async-start | bytes 14155776 | tf_op jit(solution)/shard_map/psum | solution.py:37
  783.7 16.3 %copy-start.37 = (bf16[3,577,192]{1,2,0:T(8,128)(2,1)S(1)}, bf16[3,577,192]{1,2,0:T(8,128)(2,1)}, u32[]{:S(2)}) copy-start(bf16[3,577,192]{1,2,0:T(8,128)(2,1)} %param.15) | copy-start | bytes 1994116
  786.2 15.2 %copy-start.97 = (f32[192]{0:T(256)S(1)}, f32[192]{0:T(256)}, u32[]{:S(2)}) copy-start(f32[192]{0:T(256)} %get-tuple-element.22) | copy-start | bytes 2308
  786.2 15.2 %copy-start.98 = (f32[192]{0:T(256)S(1)}, f32[192]{0:T(256)}, u32[]{:S(2)}) copy-start(f32[192]{0:T(256)} %get-tuple-element.42) | copy-start | bytes 2308
  786.2 15.2 %copy-start.99 = (f32[192]{0:T(256)S(1)}, f32[192]{0:T(256)}, u32[]{:S(2)}) copy-start(f32[192]{0:T(256)} %get-tuple-element.20) | copy-start | bytes 2308
  786.2 15.2 %copy-start.100 = (f32[192]{0:T(256)S(1)}, f32[192]{0:T(256)}, u32[]{:S(2)}) copy-start(f32[192]{0:T(256)} %get-tuple-element.41) | copy-start | bytes 2308
  786.3 98.1 %copy-start.31 = (f32[577,192]{0,1:T(8,128)S(1)}, f32[577,192]{0,1:T(8,128)}, u32[]{:S(2)}) copy-start(f32[577,192]{0,1:T(8,128)} %copy-done.30) | copy-start | bytes 1329412
  788.5 97.1 %copy-start.63 = (f32[577,192]{0,1:T(8,128)S(1)}, f32[577,192]{0,1:T(8,128)}, u32[]{:S(2)}) copy-start(f32[577,192]{0,1:T(8,128)} %get-tuple-element.83) | copy-start | bytes 1329412
  (113 other events, 262.1 us)
Sparse Core Ops, SparseCore 0:
  35.6 38.2 reduce-scatter.12
  97.2 36.4 reduce-scatter.14
  161.5 39.6 reduce-scatter.16
  224.3 36.3 reduce-scatter.18
  291.7 38.7 reduce-scatter.20
  354.7 36.3 reduce-scatter.24
  429.3 36.4 reduce-scatter.26
  469.2 36.8 reduce-scatter.22
  539.9 37.0 reduce-scatter.28
  613.3 36.4 reduce-scatter.30
  691.1 37.1 reduce-scatter.32
  763.6 36.4 reduce-scatter.34
  805.0 129.3 all-reduce.9
where the time goes:
time: 955 us; the launch traced here: 949 us
  waiting for transfers between devices  456 us (48%)
  blocking collectives  263 us (28%)
  matrix products  110 us (12%)
  other arithmetic  54.8 us (6%)
  local copies, waits for them, and re-layouts  36.3 us (4%)
  between operations  19.7 us (2%)
  starting transfers between devices  9.81 us (1%)
    reduce_scatter x3, waiting for transfers between devices, layer_backward(): lax.psum_scatter(contract_cols(pre_grad, up_mat), 'tensor', scatter_dimen...  106 us
    reduce_scatter x3, waiting for transfers between devices, layer_forward(): lax.psum_scatter(jnp.dot(attended, out_mat, preferred_element_type=jnp.fl...  102 us
    reduce_scatter x3, waiting for transfers between devices, layer_forward(): lax.psum_scatter(jnp.dot(hidden, down_mat, preferred_element_type=jnp.flo...  101 us
    reduce_scatter x3, waiting for transfers between devices, layer_backward(): lax.psum_scatter(contract_cols(flat_grad, qkv_mat.reshape(hidden_width, 3...  79.2 us
    psum x1, blocking collectives, member_sum(): return lax.psum(gradients, 'dp')  62.2 us
    psum x1, waiting for transfers between devices, member_sum(): return lax.psum(gradients, 'dp')  46.2 us
    all_gather x3, blocking collectives, layer_backward(): lax.all_gather(middle_grad.astype(jnp.bfloat16), 'tensor', axis=1, tiled=...  36.8 us
    all_gather x3, blocking collectives, layer_forward(): lax.all_gather(partial_residual, 'tensor', axis=1, tiled=True)  36.7 us
  transfers between devices with their start and end apart: 17, of which 17 were waited for; matrix products, arithmetic and copies ran while one was open for 5% of the time, Pallas kernels for 0%

commit v1 on v0

--- a/solution.py
+++ b/solution.py
@@ -177,7 +177,12 @@
     def local_part(vector):
         return lax.dynamic_slice_in_dim(vector, column, part_width, 0)
 
-    grad_full = lax.all_gather(grad_part.astype(jnp.bfloat16), "tensor", axis=1, tiled=True)
+    grad_full = jnp.concatenate(
+        lax.all_to_all(
+            jnp.stack([grad_part.astype(jnp.bfloat16)] * lax.axis_size("tensor")), "tensor", 0, 0
+        ),
+        axis=1,
+    )
     down_grad = contract_rows(hidden, grad_full)
     down_add_grad = jnp.sum(grad_part, axis=0)
     hidden_grad = contract_cols(grad_full, down_mat)

time: 955 us -> 972 us (1.018)
    all_to_all x0 -> x2, blocking collectives: none -> 37.7 us  [layer_backward(): lax.all_to_all(jnp.stack([grad_part.astype(jnp.bfloat16)] * lax.axis_size...]
    all_gather x3 -> x0, blocking collectives: 34.4 us -> none  [layer_backward(): lax.all_gather(grad_part.astype(jnp.bfloat16), 'tensor', axis=1, tiled=True)]
  transfers between devices with their start and end apart: 17 -> 18, of which waited for: 17 -> 17; matrix products, arithmetic and copies ran while one was open for 5% -> 5% of each run, Pallas kernels for 0% -> 0%
where the time goes in v1:
time: 972 us; the launch traced here: 966 us
  waiting for transfers between devices  461 us (47%)
  blocking collectives  266 us (27%)
  matrix products  113 us (12%)
  other arithmetic  54.3 us (6%)
  local copies, waits for them, and re-layouts  37.9 us (4%)
  between operations  19.7 us (2%)
  starting transfers between devices  14 us (1%)
    reduce_scatter x3, waiting for transfers between devices, layer_forward(): lax.psum_scatter(jnp.dot(attended, out_mat, preferred_element_type=jnp.fl...  108 us
    reduce_scatter x3, waiting for transfers between devices, layer_backward(): lax.psum_scatter(contract_cols(pre_grad, up_mat), 'tensor', scatter_dimen...  105 us
    reduce_scatter x3, waiting for transfers between devices, layer_forward(): lax.psum_scatter(jnp.dot(hidden, down_mat, preferred_element_type=jnp.flo...  101 us
    reduce_scatter x3, waiting for transfers between devices, layer_backward(): lax.psum_scatter(contract_cols(flat_grad, qkv_mat.reshape(hidden_width, 3...  79.1 us
    psum x1, blocking collectives, member_sum(): return lax.psum(gradients, 'dp')  62.1 us
    psum x1, waiting for transfers between devices, member_sum(): return lax.psum(gradients, 'dp')  46.4 us
    all_to_all x2, blocking collectives, layer_backward(): lax.all_to_all(jnp.stack([grad_part.astype(jnp.bfloat16)] * lax.axis_size...  37.7 us
    all_gather x3, blocking collectives, layer_backward(): lax.all_gather(middle_grad.astype(jnp.bfloat16), 'tensor', axis=1, tiled=...  36.8 us
  transfers between devices with their start and end apart: 18, of which 17 were waited for; matrix products, arithmetic and copies ran while one was open for 5% of the time, Pallas kernels for 0%

profile of v1, /device:TPU:1, one launch (start us, length us, event | category | flops | bytes accessed | tf_op | source)
XLA Modules:
  0.0 965.6 jit_solution(17058514203149225484)
XLA Ops:
  10.3 13.4 %all-gather = bf16[1,577,768]{1,2,0:T(8,128)(2,1)S(1)} all-gather(bf16[1,577,192]{1,2,0:T(8,128)(2,1)S(1)} %dynamic-slice_select_fusion.1), channel_id=2, replica_groups=mesh['section'=2,'dp'=16,'tensor'=4] {'tensor'}, dimensions={2}, use_global_device_ids=true | all-gather | bytes 1107840 | tf_op jit(solution)/shard_map/all_gather | solution.py:63
  30.3 3.3 convolution_convert_fusion.5
  36.4 37.5 %reduce-scatter.13.cloned.1.call-done = f32[577,192]{0,1:T(8,128)} async-done(((f32[577,768]{0,1:T(8,128)}), f32[577,192]{0,1:T(8,128)}) %reduce-scatter.13.cloned.1.call-update) | async-done | bytes 443152 | tf_op jit(solution)/shard_map/reduce_scatter | solution.py:95
  75.1 11.5 %all_gather.28 = bf16[577,768]{0,1:T(8,128)(2,1)S(1)} all-gather(bf16[577,192]{0,1:T(8,128)(2,1)S(1)} %fusion.151), channel_id=1, replica_groups=mesh['section'=2,'dp'=16,'tensor'=4] {'tensor'}, dimensions={1}, use_global_device_ids=true | all-gather | bytes 1107840 | tf_op jit(solution)/shard_map/all_gather | solution.py:102
  87.1 6.5 multiply_convert_fusion.5
  97.9 35.7 %reduce-scatter.15.cloned.1.call-done = f32[577,192]{0,1:T(8,128)} async-done(((f32[577,768]{0,1:T(8,128)}), f32[577,192]{0,1:T(8,128)}) %reduce-scatter.15.cloned.1.call-update) | async-done | bytes 443152 | tf_op jit(solution)/shard_map/reduce_scatter | solution.py:113
  138.6 3.3 collective-permute-done
  141.9 11.7 %all_gather.29 = bf16[577,768]{0,1:T(8,128)(2,1)S(1)} all-gather(bf16[577,192]{0,1:T(8,128)(2,1)S(1)} %bitcast_select_fusion.3), channel_id=1, replica_groups=mesh['section'=2,'dp'=16,'tensor'=4] {'tensor'}, dimensions={1}, use_global_device_ids=true | all-gather | bytes 1107840 | tf_op jit(solution)/shard_map/all_gather | solution.py:63
  161.4 39.7 %reduce-scatter.17.cloned.1.call-done = f32[577,192]{0,1:T(8,128)} async-done(((f32[577,768]{0,1:T(8,128)}), f32[577,192]{0,1:T(8,128)}) %reduce-scatter.17.cloned.1.call-update) | async-done | bytes 443152 | tf_op jit(solution)/shard_map/reduce_scatter | solution.py:95
  202.2 11.3 %all_gather.30 = bf16[577,768]{0,1:T(8,128)(2,1)S(1)} all-gather(bf16[577,192]{0,1:T(8,128)(2,1)S(1)} %fusion.153), channel_id=1, replica_groups=mesh['section'=2,'dp'=16,'tensor'=4] {'tensor'}, dimensions={1}, use_global_device_ids=true | all-gather | bytes 1107840 | tf_op jit(solution)/shard_map/all_gather | solution.py:102
  214.1 6.5 multiply_convert_fusion.4
  224.6 36.1 %reduce-scatter.19.cloned.1.call-done = f32[577,192]{0,1:T(8,128)} async-done(((f32[577,768]{0,1:T(8,128)}), f32[577,192]{0,1:T(8,128)}) %reduce-scatter.19.cloned.1.call-update) | async-done | bytes 443152 | tf_op jit(solution)/shard_map/reduce_scatter | solution.py:113
  266.3 3.6 collective-permute-done.1
  271.6 11.6 %all_gather.31 = bf16[577,768]{0,1:T(8,128)(2,1)S(1)} all-gather(bf16[577,192]{0,1:T(8,128)(2,1)S(1)} %bitcast_select_fusion.2), channel_id=1, replica_groups=mesh['section'=2,'dp'=16,'tensor'=4] {'tensor'}, dimensions={1}, use_global_device_ids=true | all-gather | bytes 1107840 | tf_op jit(solution)/shard_map/all_gather | solution.py:63
  294.8 4.4 all-to-all-start
  299.2 31.2 %reduce-scatter.21.cloned.1.call-done = f32[577,192]{0,1:T(8,128)} async-done(((f32[577,768]{0,1:T(8,128)}), f32[577,192]{0,1:T(8,128)}) %reduce-scatter.21.cloned.1.call-update) | async-done | bytes 443152 | tf_op jit(solution)/shard_map/reduce_scatter | solution.py:95
  331.6 11.3 %all_gather.32 = bf16[577,768]{0,1:T(8,128)(2,1)S(1)} all-gather(bf16[577,192]{0,1:T(8,128)(2,1)S(1)} %fusion.152), channel_id=1, replica_groups=mesh['section'=2,'dp'=16,'tensor'=4] {'tensor'}, dimensions={1}, use_global_device_ids=true | all-gather | bytes 1107840 | tf_op jit(solution)/shard_map/all_gather | solution.py:102
  343.8 6.8 multiply_convert_fusion.3
  350.7 4.7 convert_reduce_fusion.8
  359.5 35.8 %reduce-scatter.25.cloned.1.call-done = f32[577,192]{0,1:T(8,128)} async-done(((f32[577,768]{0,1:T(8,128)}), f32[577,192]{0,1:T(8,128)}) %reduce-scatter.25.cloned.1.call-update) | async-done | bytes 443152 | tf_op jit(solution)/shard_map/reduce_scatter | solution.py:193
  397.8 8.0 all-reduce.7
  408.7 12.2 %all_gather.33 = bf16[577,768]{0,1:T(8,128)(2,1)S(1)} all-gather(bf16[577,192]{0,1:T(8,128)(2,1)S(1)} %convert_element_type.417), channel_id=1, replica_groups=mesh['section'=2,'dp'=16,'tensor'=4] {'tensor'}, dimensions={1}, use_global_device_ids=true | all-gather | bytes 1107840 | tf_op jit(solution)/shard_map/all_gather | solution.py:224
  421.9 3.6 multiply_reduce_fusion.2
  433.4 4.0 fusion.65
  438.2 31.7 %reduce-scatter.27.cloned.1.call-done = f32[577,192]{0,1:T(8,128)} async-done(((f32[577,768]{0,1:T(8,128)}), f32[577,192]{0,1:T(8,128)}) %reduce-scatter.27.cloned.1.call-update) | async-done | bytes 443152 | tf_op jit(solution)/shard_map/reduce_scatter | solution.py:271
  472.4 8.0 all-reduce.6
  481.1 29.2 %reduce-scatter.23.cloned.1.call-done = f32[577,192]{0,1:T(8,128)} async-done(((f32[577,768]{0,1:T(8,128)}), f32[577,192]{0,1:T(8,128)}) %reduce-scatter.23.cloned.1.call-update) | async-done | bytes 443152 | tf_op jit(solution)/shard_map/reduce_scatter | solution.py:113
  515.0 7.1 collective-permute-done.2
  524.7 18.6 %all_to_all.15 = bf16[4,577,192]{1,2,0:T(8,128)(2,1)S(1)} all-to-all(bf16[4,577,192]{1,2,0:T(8,128)(2,1)S(1)} %stack.62), channel_id=1, replica_groups=mesh['section'=2,'dp'=16,'tensor'=4] {'tensor'}, dimensions={0} | all-to-all | bytes 1772544 | tf_op jit(solution)/shard_map/all_to_all | solution.py:181
  543.3 3.9 convert_reduce_fusion.7
  550.7 36.5 %reduce-scatter.29.cloned.1.call-done = f32[577,192]{0,1:T(8,128)} async-done(((f32[577,768]{0,1:T(8,128)}), f32[577,192]{0,1:T(8,128)}) %reduce-scatter.29.cloned.1.call-update) | async-done | bytes 443152 | tf_op jit(solution)/shard_map/reduce_scatter | solution.py:193
  589.1 7.3 all-reduce.5
  598.5 12.5 %all_gather.34 = bf16[577,768]{0,1:T(8,128)(2,1)S(1)} all-gather(bf16[577,192]{0,1:T(8,128)(2,1)S(1)} %convert_element_type.429), channel_id=1, replica_groups=mesh['section'=2,'dp'=16,'tensor'=4] {'tensor'}, dimensions={1}, use_global_device_ids=true | all-gather | bytes 1107840 | tf_op jit(solution)/shard_map/all_gather | solution.py:224
  611.9 3.6 multiply_reduce_fusion.1
  623.5 36.5 %reduce-scatter.31.cloned.1.call-done = f32[577,192]{0,1:T(8,128)} async-done(((f32[577,768]{0,1:T(8,128)}), f32[577,192]{0,1:T(8,128)}) %reduce-scatter.31.cloned.1.call-update) | async-done | bytes 443152 | tf_op jit(solution)/shard_map/reduce_scatter | solution.py:271
  661.9 7.3 all-reduce.4
  673.4 7.1 collective-permute-done.3
  682.6 19.1 %all_to_all.16 = bf16[4,577,192]{1,2,0:T(8,128)(2,1)S(1)} all-to-all(bf16[4,577,192]{1,2,0:T(8,128)(2,1)S(1)} %stack.64), channel_id=1, replica_groups=mesh['section'=2,'dp'=16,'tensor'=4] {'tensor'}, dimensions={0} | all-to-all | bytes 1772544 | tf_op jit(solution)/shard_map/all_to_all | solution.py:181
  701.7 3.9 convert_reduce_fusion.6
  709.1 4.1 fusion.193
  713.1 32.5 %reduce-scatter.33.cloned.1.call-done = f32[577,192]{0,1:T(8,128)} async-done(((f32[577,768]{0,1:T(8,128)}), f32[577,192]{0,1:T(8,128)}) %reduce-scatter.33.cloned.1.call-update) | async-done | bytes 443152 | tf_op jit(solution)/shard_map/reduce_scatter | solution.py:193
  746.9 7.3 all-reduce.3
  755.8 12.1 %all_gather.35 = bf16[577,768]{0,1:T(8,128)(2,1)S(1)} all-gather(bf16[577,192]{0,1:T(8,128)(2,1)S(1)} %convert_element_type.441), channel_id=1, replica_groups=mesh['section'=2,'dp'=16,'tensor'=4] {'tensor'}, dimensions={1}, use_global_device_ids=true | all-gather | bytes 1107840 | tf_op jit(solution)/shard_map/all_gather | solution.py:224
  768.8 3.6 multiply_reduce_fusion
  806.0 10.9 %reduce-scatter.35.cloned.1.call-done = f32[577,192]{0,1:T(8,128)} async-done(((f32[577,768]{0,1:T(8,128)}), f32[577,192]{0,1:T(8,128)}) %reduce-scatter.35.cloned.1.call-update) | async-done | bytes 443152 | tf_op jit(solution)/shard_map/reduce_scatter | solution.py:271
  818.2 62.1 %all-reduce = (f32[1,192]{1,0:T(1,128)}, f32[1,192]{1,0:T(1,128)}, f32[1,2,192]{2,1,0:T(2,128)}, f32[1,192]{1,0:T(1,128)}, f32[1,192]{1,0:T(1,128)}, /*index=5*/...) all-reduce(f32[1,192]{1,0:T(1,128)S(1)} %bitcast.379, ...), channel_id=1, replica_groups=mesh['section'=2,'dp'=16,'tensor'=4] {'dp'}, use_global_device_ids=true, to_apply=%region_60.61 | all-reduce | flops 2304 | bytes 18432 | tf_op jit(solution)/shard_map/psum | solution.py:37
  880.4 20.7 %all-reduce.2 = (f32[577]{0:T(1024)S(1)}, f32[577,1]{0,1:T(1,128)S(1)}) all-reduce(f32[577]{0:T(1024)S(1)} %get-tuple-element.25, f32[577,1]{0,1:T(1,128)S(1)} %broadcast_in_dim.58), channel_id=1, replica_groups=mesh['section'=2,'dp'=16,'tensor'=4] {'tensor'}, use_global_device_ids=true, to_apply=%region_56.57 | all-reduce | flops 1154 | bytes 9232 | tf_op jit(solution)/shard_map/psum | solution.py:283
  904.8 46.4 %all-reduce.10.cloned.1.call-done = (f32[1,768,3,192]{1,3,2,0:T(8,128)}, f32[1,192,768]{2,1,0:T(8,128)}, f32[1,768,768]{2,1,0:T(8,128)}, f32[1,768,768]{2,1,0:T(8,128)}) async-done(((f32[1,768,3,192]{1,3,2,0:T(8,128)}, f32[1,192,768]{2,1,0:T(8,128)}, f32[1,768,768]{2,1,0:T(8,128)}, f32[1,768,768]{2,1,0:T(8,128)}), (f32[1,768,3,192]{1,3,2,0:T(8,128)}, f32[1,192,768]{2,1,0:T(8,128)}, ...) | async-done | bytes 7077904 | tf_op jit(solution)/shard_map/psum | solution.py:37
  (484 shorter events, 160.3 us)
Async XLA Ops:
  7.2 79.9 %copy-start = (bf16[1,768,768]{2,1,0:T(8,128)(2,1)S(1)}, bf16[1,768,768]{2,1,0:T(8,128)(2,1)}, u32[]{:S(2)}) copy-start(bf16[1,768,768]{2,1,0:T(8,128)(2,1)} %param.25) | copy-start | bytes 3538948
  7.2 66.8 %reduce-scatter.13.cloned.1.call-start = ((), (), s32[]{:S(2)}) async-start(), calls=%async_computation.15 | async-start | bytes 2457600 | tf_op jit(solution)/shard_map/reduce_scatter | solution.py:95
  9.3 14.9 %copy-start.92 = (f32[1,768]{1,0:T(1,128)S(1)}, f32[1,768]{1,0:T(1,128)}, u32[]{:S(2)}) copy-start(f32[1,768]{1,0:T(1,128)} %param.17) | copy-start | bytes 9220
  9.3 14.9 %copy-start.118 = (f32[1,768]{1,0:T(1,128)S(1)}, f32[1,768]{1,0:T(1,128)}, u32[]{:S(2)}) copy-start(f32[1,768]{1,0:T(1,128)} %param.18) | copy-start | bytes 9220
  24.2 259.5 %copy-start.100 = (f32[768]{0:T(1024)}, f32[768]{0:T(1024)S(1)}, u32[]{:S(2)}) copy-start(f32[768]{0:T(1024)S(1)} %reduce.8) | copy-start | bytes 9220
  24.3 129.9 %copy-start.102 = (f32[768]{0:T(1024)}, f32[768]{0:T(1024)S(1)}, u32[]{:S(2)}) copy-start(f32[768]{0:T(1024)S(1)} %reduce.9) | copy-start | bytes 9220
  33.7 40.3 %copy-start.36 = (bf16[3,577,192]{1,2,0:T(8,128)(2,1)S(1)}, bf16[3,577,192]{1,2,0:T(8,128)(2,1)}, u32[]{:S(2)}) copy-start(bf16[3,577,192]{1,2,0:T(8,128)(2,1)} %param.15) | copy-start | bytes 1994116
  35.5 98.1 %reduce-scatter.15.cloned.1.call-start = ((), (), s32[]{:S(2)}) async-start(), calls=%async_computation.16 | async-start | bytes 2457600 | tf_op jit(solution)/shard_map/reduce_scatter | solution.py:113
  35.6 178.4 %copy-start.105 = (f32[768]{0:T(1024)}, f32[768]{0:T(1024)S(1)}, u32[]{:S(2)}) copy-start(f32[768]{0:T(1024)S(1)} %reduce.14) | copy-start | bytes 9220
  97.0 104.1 %reduce-scatter.17.cloned.1.call-start = ((), (), s32[]{:S(2)}) async-start(), calls=%async_computation.17 | async-start | bytes 2457600 | tf_op jit(solution)/shard_map/reduce_scatter | solution.py:95
  134.9 6.9 collective-permute-start
  141.9 59.2 %copy-start.6 = (bf16[577,192]{0,1:T(8,128)(2,1)}, bf16[577,192]{0,1:T(8,128)(2,1)S(1)}, u32[]{:S(2)}) copy-start(bf16[577,192]{0,1:T(8,128)(2,1)S(1)} %bitcast_select_fusion.3) | copy-start | bytes 664708
  141.9 12.3 %copy-start.126 = (bf16[1,768,3,192]{1,3,2,0:T(8,128)(2,1)S(1)}, bf16[1,768,3,192]{1,3,2,0:T(8,128)(2,1)}, u32[]{:S(2)}) copy-start(bf16[1,768,3,192]{1,3,2,0:T(8,128)(2,1)} %param.19) | copy-start | bytes 2654212
  161.3 99.3 %reduce-scatter.19.cloned.1.call-start = ((), (), s32[]{:S(2)}) async-start(), calls=%async_computation.18 | async-start | bytes 2457600 | tf_op jit(solution)/shard_map/reduce_scatter | solution.py:113
  224.1 106.3 %reduce-scatter.21.cloned.1.call-start = ((), (), s32[]{:S(2)}) async-start(), calls=%async_computation.19 | async-start | bytes 2457600 | tf_op jit(solution)/shard_map/reduce_scatter | solution.py:95
  262.7 7.2 collective-permute-start.1
  271.6 12.1 %copy-start.127 = (bf16[1,768,3,192]{1,3,2,0:T(8,128)(2,1)S(1)}, bf16[1,768,3,192]{1,3,2,0:T(8,128)(2,1)}, u32[]{:S(2)}) copy-start(bf16[1,768,3,192]{1,3,2,0:T(8,128)(2,1)} %param.19) | copy-start | bytes 2654212
  294.8 55.8 %all-to-all-start = ((bf16[4,577,192]{1,2,0:T(8,128)(2,1)}), bf16[4,577,192]{1,2,0:T(8,128)(2,1)}, u32[]{:S(2)}, u32[]{:S(2)}) async-start(bf16[4,577,192]{1,2,0:T(8,128)(2,1)} %stack.60), calls=%async_computation.6 | async-start | bytes 1966080 | tf_op jit(solution)/shard_map/all_to_all | solution.py:181
  299.2 96.1 %reduce-scatter.25.cloned.1.call-start = ((), (), s32[]{:S(2)}) async-start(), calls=%async_computation.21 | async-start | bytes 2457600 | tf_op jit(solution)/shard_map/reduce_scatter | solution.py:193
  331.6 12.3 %copy-start.106 = (f32[768]{0:T(1024)S(1)}, f32[768]{0:T(1024)}, u32[]{:S(2)}) copy-start(f32[768]{0:T(1024)} %copy-done.105) | copy-start | bytes 9220
  358.7 111.2 %reduce-scatter.27.cloned.1.call-start = ((), (), s32[]{:S(2)}) async-start(), calls=%async_computation.22 | async-start | bytes 2457600 | tf_op jit(solution)/shard_map/reduce_scatter | solution.py:271
  408.7 12.7 %copy-start.20 = (f32[577,192]{0,1:T(8,128)}, f32[577,192]{0,1:T(8,128)S(1)}, u32[]{:S(2)}) copy-start(f32[577,192]{0,1:T(8,128)S(1)} %get-tuple-element.77) | copy-start | bytes 1329412
  408.7 13.2 %copy-start.35 = (f32[577,1,192]{0,2,1:T(8,128)S(1)}, f32[577,1,192]{0,2,1:T(8,128)}, u32[]{:S(2)}) copy-start(f32[577,1,192]{0,2,1:T(8,128)} %copy-done.34) | copy-start | bytes 1329412
  433.3 76.9 %reduce-scatter.23.cloned.1.call-start = ((), (), s32[]{:S(2)}) async-start(), calls=%async_computation.20 | async-start | bytes 2457600 | tf_op jit(solution)/shard_map/reduce_scatter | solution.py:113
  437.4 149.8 %reduce-scatter.29.cloned.1.call-start = ((), (), s32[]{:S(2)}) async-start(), calls=%async_computation.23 | async-start | bytes 2457600 | tf_op jit(solution)/shard_map/reduce_scatter | solution.py:193
  513.1 9.0 collective-permute-start.2
  524.6 18.7 %copy-start.108 = (f32[768]{0:T(1024)S(1)}, f32[768]{0:T(1024)}, u32[]{:S(2)}) copy-start(f32[768]{0:T(1024)} %copy-done.105) | copy-start | bytes 9220
  524.6 18.7 %copy-start.124 = (bf16[1,768,768]{2,1,0:T(8,128)(2,1)S(1)}, bf16[1,768,768]{2,1,0:T(8,128)(2,1)}, u32[]{:S(2)}) copy-start(bf16[1,768,768]{2,1,0:T(8,128)(2,1)} %param.27) | copy-start | bytes 3538948
  524.6 18.7 %copy-start.137 = (f32[577,768]{1,0:T(8,128)S(1)}, f32[577,768]{1,0:T(8,128)}, u32[]{:S(2)}) copy-start(f32[577,768]{1,0:T(8,128)} %get-tuple-element.87) | copy-start | bytes 5317636
  550.6 109.3 %reduce-scatter.31.cloned.1.call-start = ((), (), s32[]{:S(2)}) async-start(), calls=%async_computation.24 | async-start | bytes 2457600 | tf_op jit(solution)/shard_map/reduce_scatter | solution.py:271
  598.4 12.9 %copy-start.21 = (f32[577,192]{0,1:T(8,128)}, f32[577,192]{0,1:T(8,128)S(1)}, u32[]{:S(2)}) copy-start(f32[577,192]{0,1:T(8,128)S(1)} %get-tuple-element.75) | copy-start | bytes 1329412
  598.4 13.5 %copy-start.29 = (f32[577,1,192]{0,2,1:T(8,128)S(1)}, f32[577,1,192]{0,2,1:T(8,128)}, u32[]{:S(2)}) copy-start(f32[577,1,192]{0,2,1:T(8,128)} %copy-done.28) | copy-start | bytes 1329412
  623.4 122.2 %reduce-scatter.33.cloned.1.call-start = ((), (), s32[]{:S(2)}) async-start(), calls=%async_computation.25 | async-start | bytes 2457600 | tf_op jit(solution)/shard_map/reduce_scatter | solution.py:193
  671.6 8.9 collective-permute-start.3
  682.4 19.2 %copy-start.109 = (f32[768]{0:T(1024)S(1)}, f32[768]{0:T(1024)}, u32[]{:S(2)}) copy-start(f32[768]{0:T(1024)} %copy-done.105) | copy-start | bytes 9220
  682.4 19.2 %copy-start.125 = (bf16[1,768,768]{2,1,0:T(8,128)(2,1)S(1)}, bf16[1,768,768]{2,1,0:T(8,128)(2,1)}, u32[]{:S(2)}) copy-start(bf16[1,768,768]{2,1,0:T(8,128)(2,1)} %param.27) | copy-start | bytes 3538948
  682.4 19.2 %copy-start.136 = (f32[577,768]{1,0:T(8,128)S(1)}, f32[577,768]{1,0:T(8,128)}, u32[]{:S(2)}) copy-start(f32[577,768]{1,0:T(8,128)} %get-tuple-element.89) | copy-start | bytes 5317636
  709.0 107.9 %reduce-scatter.35.cloned.1.call-start = ((), (), s32[]{:S(2)}) async-start(), calls=%async_computation.26 | async-start | bytes 2457600 | tf_op jit(solution)/shard_map/reduce_scatter | solution.py:271
  755.7 12.5 %copy-start.30 = (f32[577,192]{0,1:T(8,128)}, f32[577,192]{0,1:T(8,128)S(1)}, u32[]{:S(2)}) copy-start(f32[577,192]{0,1:T(8,128)S(1)} %get-tuple-element.79) | copy-start | bytes 1329412
  755.8 13.1 %copy-start.25 = (f32[577,1,192]{0,2,1:T(8,128)S(1)}, f32[577,1,192]{0,2,1:T(8,128)}, u32[]{:S(2)}) copy-start(f32[577,1,192]{0,2,1:T(8,128)} %copy-done.24) | copy-start | bytes 1329412
  780.3 170.8 %all-reduce.10.cloned.1.call-start = ((), (), s32[]{:S(2)}) async-start(), calls=%async_computation.27 | async-start | bytes 14155776 | tf_op jit(solution)/shard_map/psum | solution.py:37
  800.6 16.3 %copy-start.37 = (bf16[3,577,192]{1,2,0:T(8,128)(2,1)S(1)}, bf16[3,577,192]{1,2,0:T(8,128)(2,1)}, u32[]{:S(2)}) copy-start(bf16[3,577,192]{1,2,0:T(8,128)(2,1)} %param.15) | copy-start | bytes 1994116
  803.2 15.0 %copy-start.96 = (f32[192]{0:T(256)S(1)}, f32[192]{0:T(256)}, u32[]{:S(2)}) copy-start(f32[192]{0:T(256)} %get-tuple-element.22) | copy-start | bytes 2308
  803.2 15.0 %copy-start.97 = (f32[192]{0:T(256)S(1)}, f32[192]{0:T(256)}, u32[]{:S(2)}) copy-start(f32[192]{0:T(256)} %get-tuple-element.42) | copy-start | bytes 2308
  803.2 15.0 %copy-start.98 = (f32[192]{0:T(256)S(1)}, f32[192]{0:T(256)}, u32[]{:S(2)}) copy-start(f32[192]{0:T(256)} %get-tuple-element.20) | copy-start | bytes 2308
  803.2 15.0 %copy-start.99 = (f32[192]{0:T(256)S(1)}, f32[192]{0:T(256)}, u32[]{:S(2)}) copy-start(f32[192]{0:T(256)} %get-tuple-element.41) | copy-start | bytes 2308
  803.2 97.9 %copy-start.31 = (f32[577,192]{0,1:T(8,128)S(1)}, f32[577,192]{0,1:T(8,128)}, u32[]{:S(2)}) copy-start(f32[577,192]{0,1:T(8,128)} %copy-done.30) | copy-start | bytes 1329412
  805.4 96.9 %copy-start.63 = (f32[577,192]{0,1:T(8,128)S(1)}, f32[577,192]{0,1:T(8,128)}, u32[]{:S(2)}) copy-start(f32[577,192]{0,1:T(8,128)} %get-tuple-element.83) | copy-start | bytes 1329412
  (114 other events, 274.2 us)
Sparse Core Ops, SparseCore 0:
  35.6 38.3 reduce-scatter.12
  97.2 36.3 reduce-scatter.14
  161.4 39.6 reduce-scatter.16
  224.2 36.4 reduce-scatter.18
  291.6 38.7 reduce-scatter.20
  358.8 36.4 reduce-scatter.24
  433.5 36.4 reduce-scatter.26
  473.4 36.8 reduce-scatter.22
  550.8 36.3 reduce-scatter.28
  623.5 36.4 reduce-scatter.30
  709.1 36.4 reduce-scatter.32
  780.4 36.3 reduce-scatter.34
  821.8 129.3 all-reduce.9
